TPU v7x, 128 devices: a whole 4x4x4 slice. The times are simulated.
128 devices in a mesh: leaf: 4 (over x_lo, core), row: 8 (over x_hi, y), col: 4 (over z).
Axes of the slice: x: 4 (x_hi: 2, x_lo: 2; x = x_hi * 2 + x_lo), y: 4, z: 4, core: 2. Of those that a mesh axis runs over, the one named last changes fastest.
Arguments:
- parent_adj: float32 [16384, 16384], P(('leaf', 'row'), 'col'), may hold values from -70 to 70, as said below
- child_map: int32 [4, 8], replicated, may hold values from 0 to 127, as said below
- lower_panel: float32 [4, 1024, 4096], P('leaf', 'col', 'row'), may hold values from -0.09375 to 0.09375
- pivot_inverse: float32 [4, 4096, 4096], P('leaf', 'row', 'col'), may hold values from -1 to 3, as said below
Outputs:
- update_adj: float32 [4, 1024, 1024], P('leaf', 'row', 'col')
- off_adj: float32 [4, 1024, 4096], P('leaf', 'row', 'col')
- pivot_adj: float32 [4, 4096, 4096], P('leaf', 'row', 'col')
Inputs may be any that keep to these rules, and one draw needn't show every extreme that they name: `child_map`: each row lists 8 distinct parent block ids in increasing order; every row contains block 0 and block 127. parent_adj is symmetric. Each pivot_inverse[c] is lower triangular with diagonal entries of 1 to 3.
All inputs are finite; a program needn't handle non-finite values.
Results may differ from a plain program's by a relative error of at most 0.0003.
Values sent between devices are 32-bit elements; how exact they have to be, the bound alone decides.
A program may use at most 128 MiB of HBM per device.

v0:
```python
import jax
import jax.numpy as jnp
from jax import lax
from jax.sharding import PartitionSpec as P

BLK = 128
exact_mode = lax.Precision.HIGHEST


def take_child(blocks_view, block_ids):
    return jnp.take(blocks_view, block_ids, axis=0)


def shards(parent_adj, child_map, lower_panel, pivot_inverse):
    row_count = lax.axis_size("row")
    column_count = lax.axis_size("col")
    leaf_index = lax.axis_index("leaf")
    row_index = lax.axis_index("row")
    column_index = lax.axis_index("col")
    children = child_map.shape[0]
    blocks_all = child_map.shape[1]
    local_rows = parent_adj.shape[0]
    local_columns = parent_adj.shape[1]
    row_blocks = local_rows // BLK
    column_blocks = local_columns // BLK
    per_column = blocks_all // column_count
    per_row = blocks_all // row_count
    width = per_column * BLK
    column_ids = jnp.transpose(child_map.reshape(children, column_count, per_column), (1, 0, 2))
    column_local = column_ids - column_index * column_blocks
    column_owned = (column_local >= 0) & (column_local < column_blocks)
    column_safe = jnp.clip(column_local, 0, column_blocks - 1)
    parent_view = parent_adj.reshape(local_rows, column_blocks, BLK)
    picked = jnp.take(parent_view, column_safe.reshape(-1), axis=1)
    picked = picked.reshape(local_rows, column_count, children, per_column, BLK)
    picked = jnp.where(column_owned[None, :, :, :, None], picked, 0.0)
    picked = picked.reshape(local_rows, column_count, children * width)
    columns_kept = lax.psum_scatter(picked, "col", scatter_dimension=1, tiled=True)
    selected = columns_kept.reshape(row_blocks, BLK, children, width)
    by_child = jnp.moveaxis(selected, 2, 0)
    owner = leaf_index * row_count + row_index
    row_local = child_map - owner * row_blocks
    row_owned = (row_local >= 0) & (row_local < row_blocks)
    row_safe = jnp.clip(row_local, 0, row_blocks - 1)
    contribution = jax.vmap(take_child)(by_child, row_safe)
    contribution = jnp.where(row_owned[:, :, None, None], contribution, 0.0)
    update = lax.psum_scatter(
        contribution.reshape(children * row_count * per_row * BLK, width),
        ("leaf", "row"),
        scatter_dimension=0,
        tiled=True,
    )
    lower = lower_panel[0]
    inverse = pivot_inverse[0]
    lower_all = lax.all_gather(lower, "col", axis=0, tiled=True)
    factor = lax.psum_scatter(
        jnp.dot(lower_all, inverse, precision=exact_mode, preferred_element_type=jnp.float32),
        "row",
        scatter_dimension=0,
        tiled=True,
    )
    update_all = lax.all_gather(update, "col", axis=1, tiled=True)
    carried = jnp.dot(
        update_all,
        lax.all_gather(factor, "row", axis=0, tiled=True),
        precision=exact_mode,
        preferred_element_type=jnp.float32,
    )
    factor_all, inverse_all = (
        lax.all_gather(factor, "col", axis=1, tiled=True),
        lax.all_gather(inverse, "col", axis=1, tiled=True),
    )
    first = jnp.dot(factor_all.T, carried, precision=exact_mode, preferred_element_type=jnp.float32)
    second = jnp.dot(
        inverse_all.T, inverse, precision=exact_mode, preferred_element_type=jnp.float32
    )
    pivot = lax.psum_scatter(first + second, "row", scatter_dimension=0, tiled=True)
    return (update[None], (-2.0 * carried)[None], pivot[None])


def solution(mesh):
    in_specs = (P(("leaf", "row"), "col"), P(), P("leaf", "col", "row"), P("leaf", "row", "col"))
    out_specs = (P("leaf", "row", "col"), P("leaf", "row", "col"), P("leaf", "row", "col"))
    return jax.shard_map(shards, mesh=mesh, in_specs=in_specs, out_specs=out_specs, check_vma=False)
```

profile of v0, /device:TPU:2, one launch (start us, length us, event | category | flops | bytes accessed | tf_op | source)
XLA Modules:
  0.0 789.7 jit_solution(10354824878462700312)
XLA Ops:
  7.2 0.0 all-gather.11.cloned.1.call-start
  7.2 0.7 all-gather.11.cloned.1.call-update
  7.9 0.0 reduce-scatter.5.cloned.1.call-start
  7.9 0.7 subtract_clamp_fusion
  8.6 0.1 copy.40
  8.7 0.1 copy.43
  8.8 0.1 copy.41
  9.0 0.1 broadcast_in_dim.82
  9.1 0.7 compare_and_fusion.3
  9.8 0.1 and.31
  9.9 0.1 broadcast_in_dim.79
  10.0 9.0 %copy.42 = f32[512,4096]{0,1:T(8,128)} copy(f32[512,4096]{1,0:T(8,128)} %param.4) | data formatting | bytes 16777216 | tf_op args[0]
  19.0 9.0 %copy.44 = f32[512,32,128]{2,0,1:T(8,128)} copy(f32[512,32,128]{0,2,1:T(8,128)} %bitcast.49) | data formatting | bytes 16777216 | tf_op jit(solution)/shard_map/reshape | solution.py:33
  28.0 0.1 reshape.79
  28.1 7.8 gather_fusion
  35.9 9.0 %copy.45 = f32[512,32,128]{0,2,1:T(8,128)} copy(f32[512,32,128]{2,0,1:T(8,128)} %bitcast.47) | data formatting | bytes 16777216 | tf_op jit(solution)/shard_map/jit(_take)/gather | solution.py:34
  44.9 7.4 fusion.2
  52.4 0.0 reduce-scatter.5.cloned.1.call-update
  52.4 0.0 reduce-scatter.9.cloned.1.call-start
  52.5 0.0 all-gather.11.cloned.1.call-done
  52.5 1.5 copy-done
  54.0 9.7 %fusion.5 = f32[1024,1024]{1,0:T(8,128)} fusion(f32[1,512,1024]{2,1,0:T(8,128)S(1)} %copy-done, f32[1,1024,512]{2,1,0:T(8,128)} %all-gather.11.cloned.1.call-done), kind=kOutput, calls=%fused_computation.10 | convolution fusion | flops 6442450944 | bytes 8388608 | tf_op jit(solution)/shard_map/dot_general | solution.py:57
  63.7 0.0 all-gather.13.cloned.1.call-start
  63.8 0.5 all-gather.13.cloned.1.call-update
  64.3 0.0 reduce-scatter.7.cloned.1.call-start
  64.3 0.0 copy-done.2
  64.4 0.1 reshape.89
  64.5 0.1 broadcast_bitcast_fusion
  64.5 71.2 %reduce-scatter.5.cloned.1.call-done = f32[512,1,1024]{0,2,1:T(8,128)} async-done(((f32[512,4,1024]{0,2,1:T(8,128)}), f32[512,1,1024]{0,2,1:T(8,128)}) %reduce-scatter.5.cloned.1.call-update) | async-done | bytes 2097168 | tf_op jit(solution)/shard_map/reduce_scatter | solution.py:38
  135.7 2.9 reshape.103
  138.6 1.9 copy.47
  140.5 2.8 gather_fusion.1
  143.3 6.8 fusion.3
  150.1 0.0 all-gather.7.cloned.1.call-start
  150.1 72.6 %reduce-scatter.9.cloned.1.call-done = f32[128,1024]{1,0:T(8,128)} async-done(((f32[1024,1024]{1,0:T(8,128)}), f32[128,1024]{1,0:T(8,128)}) %reduce-scatter.9.cloned.1.call-update) | async-done | bytes 524304 | tf_op jit(solution)/shard_map/reduce_scatter | solution.py:56
  222.7 0.0 all-gather.9.cloned.1.call-start
  222.8 0.7 all-gather.9.cloned.1.call-update
  223.5 0.2 reduce-scatter.11.cloned.1.call-start
  223.7 83.7 %all-gather.13.cloned.1.call-done = f32[1,512,4096]{2,1,0:T(8,128)} async-done(((f32[1,512,1024]{2,1,0:T(8,128)}), f32[1,512,4096]{2,1,0:T(8,128)}) %all-gather.13.cloned.1.call-update) | async-done | bytes 8388624 | tf_op jit(solution)/shard_map/all_gather | solution.py:71
  307.4 30.7 %fusion = f32[4096,1024]{1,0:T(8,128)} fusion(f32[1,512,4096]{2,1,0:T(8,128)} %all-gather.13.cloned.1.call-done, f32[1,512,1024]{2,1,0:T(8,128)S(1)} %copy-done.1), kind=kOutput, calls=%fused_computation.3 | convolution fusion | flops 25769803776 | bytes 27262976 | tf_op jit(solution)/shard_map/dot_general | solution.py:74
  338.1 125.8 %reduce-scatter.7.cloned.1.call-done = f32[128,256]{1,0:T(8,128)} async-done(((f32[4096,256]{1,0:T(8,128)}), f32[128,256]{1,0:T(8,128)}) %reduce-scatter.7.cloned.1.call-update) | async-done | bytes 131088 | tf_op jit(solution)/shard_map/reduce_scatter | solution.py:47
  463.9 13.5 %all_gather.15 = f32[128,1024]{1,0:T(8,128)S(1)} all-gather(f32[128,256]{1,0:T(8,128)} %reduce-scatter.7.cloned.1.call-done), channel_id=1, replica_groups=mesh['leaf'=4,'row'=8,'col'=4] {'col'}, dimensions={1}, use_global_device_ids=true | all-gather | bytes 655360 | tf_op jit(solution)/shard_map/all_gather | solution.py:62
  477.4 62.9 %all-gather.7.cloned.1.call-done = f32[1024,1024]{1,0:T(8,128)} async-done(((f32[128,1024]{1,0:T(8,128)}), f32[1024,1024]{1,0:T(8,128)}) %all-gather.7.cloned.1.call-update) | async-done | bytes 4194320 | tf_op jit(solution)/shard_map/all_gather | solution.py:65
  540.2 4.6 fusion.9
  544.8 27.1 %all-gather.9.cloned.1.call-done = f32[128,4096]{1,0:T(8,128)} async-done(((f32[128,1024]{1,0:T(8,128)}), f32[128,4096]{1,0:T(8,128)}) %all-gather.9.cloned.1.call-update) | async-done | bytes 2097168 | tf_op jit(solution)/shard_map/all_gather | solution.py:70
  571.9 19.1 %convolution_add_fusion = f32[4096,1024]{1,0:T(8,128)} fusion(f32[4096,1024]{1,0:T(8,128)} %fusion, f32[128,4096]{1,0:T(8,128)} %all-gather.9.cloned.1.call-done, f32[128,1024]{1,0:T(8,128)S(1)} %fusion.9), kind=kOutput, calls=%fused_computation.2 | convolution fusion | flops 6446645248 | bytes 36175872 | tf_op jit(solution)/shard_map/dot_general | solution.py:73
  591.0 0.8 multiply_bitcast_fusion
  591.8 191.0 %reduce-scatter.11.cloned.1.call-done = f32[512,1024]{1,0:T(8,128)} async-done(((f32[4096,1024]{1,0:T(8,128)}), f32[512,1024]{1,0:T(8,128)}) %reduce-scatter.11.cloned.1.call-update) | async-done | bytes 2097168 | tf_op jit(solution)/shard_map/reduce_scatter | solution.py:77
  (15 shorter events, 0.2 us)
Async XLA Ops:
  7.2 45.3 %all-gather.11.cloned.1.call-start = ((), (), s32[]{:S(2)}) async-start(), calls=%async_computation.10 | async-start | bytes 2621440 | tf_op jit(solution)/shard_map/all_gather | solution.py:55
  7.9 127.8 %reduce-scatter.5.cloned.1.call-start = ((), (), s32[]{:S(2)}) async-start(), calls=%async_computation.4 | async-start | bytes 10485760 | tf_op jit(solution)/shard_map/reduce_scatter | solution.py:38
  52.4 1.6 copy-start
  52.4 170.3 %reduce-scatter.9.cloned.1.call-start = ((), (), s32[]{:S(2)}) async-start(), calls=%async_computation.6 | async-start | bytes 4718592 | tf_op jit(solution)/shard_map/reduce_scatter | solution.py:56
  63.7 0.7 copy-start.2
  63.7 243.7 %all-gather.13.cloned.1.call-start = ((), (), s32[]{:S(2)}) async-start(), calls=%async_computation.11 | async-start | bytes 10485760 | tf_op jit(solution)/shard_map/all_gather | solution.py:71
  64.3 399.6 %reduce-scatter.7.cloned.1.call-start = ((), (), s32[]{:S(2)}) async-start(), calls=%async_computation.5 | async-start | bytes 4325376 | tf_op jit(solution)/shard_map/reduce_scatter | solution.py:47
  150.0 157.4 %copy-start.1 = (f32[1,512,1024]{2,1,0:T(8,128)S(1)}, f32[1,512,1024]{2,1,0:T(8,128)}, u32[]{:S(2)}) copy-start(f32[1,512,1024]{2,1,0:T(8,128)} %param.7) | copy-start | bytes 6291460
  150.1 390.2 %all-gather.7.cloned.1.call-start = ((), (), s32[]{:S(2)}) async-start(), calls=%async_computation.7 | async-start | bytes 4718592 | tf_op jit(solution)/shard_map/all_gather | solution.py:65
  222.7 349.2 %all-gather.9.cloned.1.call-start = ((), (), s32[]{:S(2)}) async-start(), calls=%async_computation.8 | async-start | bytes 2621440 | tf_op jit(solution)/shard_map/all_gather | solution.py:70
  223.5 559.4 %reduce-scatter.11.cloned.1.call-start = ((), (), s32[]{:S(2)}) async-start(), calls=%async_computation.9 | async-start | bytes 18874368 | tf_op jit(solution)/shard_map/reduce_scatter | solution.py:77
Sparse Core Ops, SparseCore 0:
  9.7 33.4 all-gather.10
  52.5 83.1 reduce-scatter.4
  139.5 83.1 reduce-scatter.8
  224.3 83.0 all-gather.12
  310.4 153.4 reduce-scatter.6
  466.4 73.7 all-gather.6
  542.0 29.8 all-gather.8
  591.1 191.6 reduce-scatter.10
where the time goes:
time: 791 us; the launch traced here: 790 us
  waiting for transfers between devices  636 us (80%)
  matrix products  64 us (8%)
  local copies, waits for them, and re-layouts  44.8 us (6%)
  other arithmetic  16.5 us (2%)
  between operations  14.2 us (2%)
  blocking collectives  13.5 us (2%)
    reduce_scatter x1, waiting for transfers between devices, shards(): lax.psum_scatter(first + second, 'row', scatter_dimension=0, tiled=True)  191 us
    reduce_scatter x1, waiting for transfers between devices, shards(): lax.psum_scatter(contribution.reshape(children * row_count * per_row * BL...  126 us
    all_gather x1, waiting for transfers between devices, shards(): lax.all_gather(inverse, 'col', axis=1, tiled=True)  83.7 us
    reduce_scatter x1, waiting for transfers between devices, shards(): lax.psum_scatter(jnp.dot(lower_all, inverse, precision=exact_mode, prefer...  72.6 us
    reduce_scatter x1, waiting for transfers between devices, shards(): lax.psum_scatter(picked, 'col', scatter_dimension=1, tiled=True)  71.2 us
    all_gather x1, waiting for transfers between devices, shards(): lax.all_gather(factor, 'row', axis=0, tiled=True)  62.9 us
    dot_general x1, matrix products, shards(): jnp.dot(inverse_all.T, inverse, precision=exact_mode, preferred_element_t...  30.7 us
    all_gather x1, waiting for transfers between devices, shards(): lax.all_gather(factor, 'col', axis=1, tiled=True)  27.1 us
  transfers between devices with their start and end apart: 8, of which 7 were waited for; matrix products, arithmetic and copies ran while one was open for 13% of the time, Pallas kernels for 0%

commit v1 on v0

--- a/solution.py
+++ b/solution.py
@@ -5,6 +5,11 @@
 
 BLK = 128
 exact_mode = lax.Precision.HIGHEST
+
+
+def tiled_gather(shard, axis, dim):
+    copies = jnp.concatenate([shard] * lax.axis_size(axis), axis=dim)
+    return lax.all_to_all(copies, axis, dim, dim, tiled=True)
 
 
 def take_child(blocks_view, block_ids):
@@ -68,7 +73,7 @@
     )
     factor_all, inverse_all = (
         lax.all_gather(factor, "col", axis=1, tiled=True),
-        lax.all_gather(inverse, "col", axis=1, tiled=True),
+        tiled_gather(inverse, "col", 1),
     )
     first = jnp.dot(factor_all.T, carried, precision=exact_mode, preferred_element_type=jnp.float32)
     second = jnp.dot(

time: 791 us -> 705 us (0.89)
  waiting for transfers between devices: 636 us -> 530 us
  local copies, waits for them, and re-layouts: 44.8 us -> 58.5 us
    reduce_scatter x1, waiting for transfers between devices: 126 us -> 12.2 us  [shards(): lax.psum_scatter(contribution.reshape(children * row_count * per_row * BL...]
    all_to_all x0 -> x1, waiting for transfers between devices: none -> 92.3 us  [tiled_gather(): return lax.all_to_all(copies, axis, dim, dim, tiled=True)]
    all_gather x1 -> x0, waiting for transfers between devices: 83.7 us -> none  [shards(): lax.all_gather(inverse, 'col', axis=1, tiled=True)]
    all_to_all x0 -> x1, local copies, waits for them, and re-layouts: none -> 8.75 us  [tiled_gather(): return lax.all_to_all(copies, axis, dim, dim, tiled=True)]
  transfers between devices with their start and end apart: 8 -> 8, of which waited for: 7 -> 7; matrix products, arithmetic and copies ran while one was open for 13% -> 17% of each run, Pallas kernels for 0% -> 0%
where the time goes in v1:
time: 705 us; the launch traced here: 704 us
  waiting for transfers between devices  530 us (75%)
  matrix products  64.4 us (9%)
  local copies, waits for them, and re-layouts  58.5 us (8%)
  other arithmetic  16.5 us (2%)
  between operations  14.2 us (2%)
  blocking collectives  13.6 us (2%)
    reduce_scatter x1, waiting for transfers between devices, shards(): lax.psum_scatter(first + second, 'row', scatter_dimension=0, tiled=True)  191 us
    all_to_all x1, waiting for transfers between devices, tiled_gather(): return lax.all_to_all(copies, axis, dim, dim, tiled=True)  92.3 us
    reduce_scatter x1, waiting for transfers between devices, shards(): lax.psum_scatter(jnp.dot(lower_all, inverse, precision=exact_mode, prefer...  72.6 us
    reduce_scatter x1, waiting for transfers between devices, shards(): lax.psum_scatter(picked, 'col', scatter_dimension=1, tiled=True)  71.2 us
    all_gather x1, waiting for transfers between devices, shards(): lax.all_gather(factor, 'row', axis=0, tiled=True)  62.8 us
    dot_general x1, matrix products, shards(): jnp.dot(inverse_all.T, inverse, precision=exact_mode, preferred_element_t...  31 us
    all_gather x1, waiting for transfers between devices, shards(): lax.all_gather(factor, 'col', axis=1, tiled=True)  26.9 us
    dot_general x1, matrix products, shards(): jnp.dot(factor_all.T, carried, precision=exact_mode, preferred_element_ty...  19.1 us
  transfers between devices with their start and end apart: 8, of which 7 were waited for; matrix products, arithmetic and copies ran while one was open for 17% of the time, Pallas kernels for 0%

profile of v1, /device:TPU:2, one launch (start us, length us, event | category | flops | bytes accessed | tf_op | source)
XLA Modules:
  0.0 703.7 jit_solution(7973748699754651959)
XLA Ops:
  7.2 0.0 all-gather.9.cloned.1.call-start
  7.2 0.7 all-gather.9.cloned.1.call-update
  7.9 0.0 reduce-scatter.5.cloned.1.call-start
  7.9 0.7 subtract_clamp_fusion
  8.6 0.1 copy.69
  8.7 0.1 copy.72
  8.8 0.1 copy.70
  9.0 0.1 broadcast_in_dim.82
  9.1 0.7 compare_and_fusion.3
  9.8 0.1 and.31
  9.9 0.1 broadcast_in_dim.79
  10.0 9.0 %copy.71 = f32[512,4096]{0,1:T(8,128)} copy(f32[512,4096]{1,0:T(8,128)} %param.4) | data formatting | bytes 16777216 | tf_op args[0]
  19.0 9.0 %copy.73 = f32[512,32,128]{2,0,1:T(8,128)} copy(f32[512,32,128]{0,2,1:T(8,128)} %bitcast.49) | data formatting | bytes 16777216 | tf_op jit(solution)/shard_map/reshape | solution.py:38
  28.0 0.1 reshape.91
  28.2 7.8 %gather_fusion = f32[32,512,128]{2,1,0:T(8,128)} fusion(f32[512,32,128]{2,0,1:T(8,128)} %copy.73, s32[1024]{0:T(1024)S(1)} %pad_clamp_fusion), kind=kCustom, calls=%fused_computation | custom fusion | bytes 16777344 | tf_op jit(solution)/shard_map/jit(_take)/gather | solution.py:39
  35.9 9.0 %copy.74 = f32[512,32,128]{0,2,1:T(8,128)} copy(f32[512,32,128]{2,0,1:T(8,128)} %bitcast.47) | data formatting | bytes 16777216 | tf_op jit(solution)/shard_map/jit(_take)/gather | solution.py:39
  44.9 7.4 %fusion = f32[512,4,1024]{0,2,1:T(8,128)} fusion(pred[4,1024]{1,0:T(4,128)(4,1)S(1)} %broadcast_in_dim.83, pred[4,1024]{1,0:T(4,128)(4,1)S(1)} %broadcast_in_dim.80, f32[512,4,1024]{0,2,1:T(8,128)} %bitcast.48), kind=kLoop, calls=%fused_computation.4 | loop fusion | flops 4194304 | bytes 16785408 | tf_op jit(solution)/shard_map/jit(_where)/select_n | solution.py:41
  52.4 0.0 reduce-scatter.9.cloned.1.call-start
  52.5 0.0 all-gather.9.cloned.1.call-done
  52.5 1.5 copy-done
  54.0 9.7 %fusion.2 = f32[1024,1024]{1,0:T(8,128)} fusion(f32[1,1024,512]{2,1,0:T(8,128)} %all-gather.9.cloned.1.call-done, f32[1,512,1024]{2,1,0:T(8,128)S(1)} %copy-done), kind=kOutput, calls=%fused_computation.7 | convolution fusion | flops 6442450944 | bytes 8388608 | tf_op jit(solution)/shard_map/dot_general | solution.py:62
  63.7 0.0 reduce-scatter.7.cloned.1.call-start
  63.8 0.6 copy-done.2
  64.4 0.1 reshape.101
  64.5 0.1 broadcast_bitcast_fusion
  64.5 71.2 %reduce-scatter.5.cloned.1.call-done = f32[512,1,1024]{0,2,1:T(8,128)} async-done(((f32[512,4,1024]{0,2,1:T(8,128)}), f32[512,1,1024]{0,2,1:T(8,128)}) %reduce-scatter.5.cloned.1.call-update) | async-done | bytes 2097168 | tf_op jit(solution)/shard_map/reduce_scatter | solution.py:43
  135.7 2.9 reshape.114
  138.6 1.9 copy.76
  140.5 2.8 gather_fusion.1
  143.3 6.8 fusion.1
  150.1 0.0 all-gather.5.cloned.1.call-start
  150.2 72.6 %reduce-scatter.9.cloned.1.call-done = f32[128,1024]{1,0:T(8,128)} async-done(((f32[1024,1024]{1,0:T(8,128)}), f32[128,1024]{1,0:T(8,128)}) %reduce-scatter.9.cloned.1.call-update) | async-done | bytes 524304 | tf_op jit(solution)/shard_map/reduce_scatter | solution.py:61
  222.8 4.3 concatenate.4
  227.1 5.6 all-to-all-start
  232.7 0.0 all-gather.7.cloned.1.call-start
  232.8 0.5 all-gather.7.cloned.1.call-update
  233.3 0.2 reduce-scatter.11.cloned.1.call-start
  233.5 92.3 %all-to-all-done = f32[512,4,1024]{2,0,1:T(8,128)} async-done(((f32[512,4,1024]{2,0,1:T(8,128)}), f32[512,4,1024]{2,0,1:T(8,128)}, u32[]{:S(2)}, u32[]{:S(2)}) %all-to-all-start) | async-done | bytes 8388640 | tf_op jit(solution)/shard_map/all_to_all | solution.py:12
  325.8 8.8 %copy.77 = f32[512,4,1024]{0,2,1:T(8,128)} copy(f32[512,4,1024]{2,0,1:T(8,128)} %all-to-all-done) | data formatting | bytes 16777216 | tf_op jit(solution)/shard_map/all_to_all | solution.py:12
  334.6 31.0 %fusion.5 = f32[4096,1024]{1,0:T(8,128)} fusion(f32[512,4096]{0,1:T(8,128)} %bitcast.46, f32[1,512,1024]{2,1,0:T(8,128)S(1)} %copy-done.1), kind=kOutput, calls=%fused_computation.23 | convolution fusion | flops 25769803776 | bytes 27262976 | tf_op jit(solution)/shard_map/dot_general | solution.py:79
  365.6 12.2 %reduce-scatter.7.cloned.1.call-done = f32[128,256]{1,0:T(8,128)} async-done(((f32[4096,256]{1,0:T(8,128)}), f32[128,256]{1,0:T(8,128)}) %reduce-scatter.7.cloned.1.call-update) | async-done | bytes 131088 | tf_op jit(solution)/shard_map/reduce_scatter | solution.py:52
  377.8 13.6 %all_gather.12 = f32[128,1024]{1,0:T(8,128)S(1)} all-gather(f32[128,256]{1,0:T(8,128)} %reduce-scatter.7.cloned.1.call-done), channel_id=1, replica_groups=mesh['leaf'=4,'row'=8,'col'=4] {'col'}, dimensions={1}, use_global_device_ids=true | all-gather | bytes 655360 | tf_op jit(solution)/shard_map/all_gather | solution.py:67
  391.5 62.8 %all-gather.5.cloned.1.call-done = f32[1024,1024]{1,0:T(8,128)} async-done(((f32[128,1024]{1,0:T(8,128)}), f32[1024,1024]{1,0:T(8,128)}) %all-gather.5.cloned.1.call-update) | async-done | bytes 4194320 | tf_op jit(solution)/shard_map/all_gather | solution.py:70
  454.3 4.6 fusion.8
  458.9 26.9 %all-gather.7.cloned.1.call-done = f32[128,4096]{1,0:T(8,128)} async-done(((f32[128,1024]{1,0:T(8,128)}), f32[128,4096]{1,0:T(8,128)}) %all-gather.7.cloned.1.call-update) | async-done | bytes 2097168 | tf_op jit(solution)/shard_map/all_gather | solution.py:75
  485.8 19.1 %convolution_add_fusion = f32[4096,1024]{1,0:T(8,128)} fusion(f32[4096,1024]{1,0:T(8,128)} %fusion.5, f32[128,4096]{1,0:T(8,128)} %all-gather.7.cloned.1.call-done, f32[128,1024]{1,0:T(8,128)S(1)} %fusion.8), kind=kOutput, calls=%fused_computation.2 | convolution fusion | flops 6446645248 | bytes 36175872 | tf_op jit(solution)/shard_map/dot_general | solution.py:78
  504.9 0.8 multiply_bitcast_fusion
  505.7 191.1 %reduce-scatter.11.cloned.1.call-done = f32[512,1024]{1,0:T(8,128)} async-done(((f32[4096,1024]{1,0:T(8,128)}), f32[512,1024]{1,0:T(8,128)}) %reduce-scatter.11.cloned.1.call-update) | async-done | bytes 2097168 | tf_op jit(solution)/shard_map/reduce_scatter | solution.py:82
  (16 shorter events, 0.2 us)
Async XLA Ops:
  7.2 45.3 %all-gather.9.cloned.1.call-start = ((), (), s32[]{:S(2)}) async-start(), calls=%async_computation.11 | async-start | bytes 2621440 | tf_op jit(solution)/shard_map/all_gather | solution.py:60
  7.9 127.8 %reduce-scatter.5.cloned.1.call-start = ((), (), s32[]{:S(2)}) async-start(), calls=%async_computation.5 | async-start | bytes 10485760 | tf_op jit(solution)/shard_map/reduce_scatter | solution.py:43
  52.4 1.6 copy-start
  52.4 170.3 %reduce-scatter.9.cloned.1.call-start = ((), (), s32[]{:S(2)}) async-start(), calls=%async_computation.7 | async-start | bytes 4718592 | tf_op jit(solution)/shard_map/reduce_scatter | solution.py:61
  63.7 0.7 copy-start.2
  63.7 314.1 %reduce-scatter.7.cloned.1.call-start = ((), (), s32[]{:S(2)}) async-start(), calls=%async_computation.6 | async-start | bytes 4325376 | tf_op jit(solution)/shard_map/reduce_scatter | solution.py:52
  150.1 72.7 %copy-start.1 = (f32[1,512,1024]{2,1,0:T(8,128)S(1)}, f32[1,512,1024]{2,1,0:T(8,128)}, u32[]{:S(2)}) copy-start(f32[1,512,1024]{2,1,0:T(8,128)} %param.7) | copy-start | bytes 6291460
  150.1 304.2 %all-gather.5.cloned.1.call-start = ((), (), s32[]{:S(2)}) async-start(), calls=%async_computation.8 | async-start | bytes 4718592 | tf_op jit(solution)/shard_map/all_gather | solution.py:70
  227.1 98.7 %all-to-all-start = ((f32[512,4,1024]{2,0,1:T(8,128)}), f32[512,4,1024]{2,0,1:T(8,128)}, u32[]{:S(2)}, u32[]{:S(2)}) async-start(f32[512,4,1024]{2,0,1:T(8,128)} %concatenate.4), calls=%async_computation.3 | async-start | bytes 16777216 | tf_op jit(solution)/shard_map/all_to_all | solution.py:12
  232.7 253.1 %all-gather.7.cloned.1.call-start = ((), (), s32[]{:S(2)}) async-start(), calls=%async_computation.9 | async-start | bytes 2621440 | tf_op jit(solution)/shard_map/all_gather | solution.py:75
  233.3 463.5 %reduce-scatter.11.cloned.1.call-start = ((), (), s32[]{:S(2)}) async-start(), calls=%async_computation.10 | async-start | bytes 18874368 | tf_op jit(solution)/shard_map/reduce_scatter | solution.py:82
Sparse Core Ops, SparseCore 0:
  9.7 33.4 all-gather.8
  52.5 83.1 reduce-scatter.4
  139.5 83.1 reduce-scatter.8
  225.7 152.0 reduce-scatter.6
  380.3 73.9 all-gather.4
  455.9 29.8 all-gather.6
  505.0 191.7 reduce-scatter.10
